TPU v7x, 256 devices: a whole 4x4x8 slice. The times are simulated.
256 devices in a mesh: case: 4 (over y_hi, core), mod: 64 (over x, y_lo, z).
Axes of the slice: x: 4, y: 4 (y_hi: 2, y_lo: 2; y = y_hi * 2 + y_lo), z: 8, core: 2. Of those that a mesh axis runs over, the one named last changes fastest.
Arguments:
- turbulence: float32 [4, 256, 256], P('case'), may hold values from -6 to 6
- pupil_amp: float32 [256, 256], replicated, may hold values from 0.3 to 1
- mod_points: int32 [64], P('mod'), may hold values from 0 to 255
- valid_pix: int32 [65536], P('mod'), may hold values from 0 to 262143, as said below
- recon: bfloat16 [5120, 65536], P('case', 'mod'), may hold values from -0.0234375 to 0.0234375
- gx: float32 [256, 64], replicated, may hold values from -1.2 to 1.2
- gy: float32 [256, 80], replicated, may hold values from -1.2 to 1.2
- act_map: int32 [5120], replicated, may hold values from 0 to 5119, each once
Outputs:
- command_total: float32 [4, 5120], P('case')
- frame: float32 [4, 512, 512], P('case', 'mod')
Inputs may be any that keep to these rules, and one draw needn't show every extreme that they name: `valid_pix`: entries k * 1024 to (k + 1) * 1024 - 1 are flat indices (row times 512 plus column) of pixels in detector rows k * 8 to (k + 1) * 8 - 1.
All inputs are finite; a program needn't handle non-finite values.
Results may differ from a plain program's by a relative error of at most 0.0058.
Values may be sent and summed in bfloat16 or wider, within the bound.
A program may use at most 64 MiB of HBM per device.

v0:
```python
import math
import jax
import jax.numpy as jnp
from jax import lax
from jax.sharding import PartitionSpec as P

STEPS = 2
loop_gain = 0.5
radius_pixels = 6.0
point_count = 256


def phase_table(length, pupil_width, sign_factor):
    centred = jnp.arange(length, dtype=jnp.int32) - length // 2
    position = jnp.arange(pupil_width, dtype=jnp.int32)
    wrapped = jnp.mod(centred[:, None] * position[None, :], length).astype(jnp.float32)
    angles = 2.0 * math.pi / length * wrapped
    factor = 1.0 / math.sqrt(length)
    return (jnp.cos(angles) * factor, sign_factor * jnp.sin(angles) * factor)


def optics_tables(pupil_size, length):
    fwd_cos, fwd_sin = phase_table(length, pupil_size, -1.0)
    inv_cos, inv_sin = phase_table(length, length, 1.0)
    inv_cos = inv_cos.T
    inv_sin = inv_sin.T
    table_one = jnp.concatenate([fwd_cos, fwd_sin], 0).astype(jnp.bfloat16)
    table_two = jnp.concatenate(
        [jnp.concatenate([fwd_cos.T, fwd_sin.T], 1), jnp.concatenate([-fwd_sin.T, fwd_cos.T], 1)], 0
    ).astype(jnp.bfloat16)
    table_three = jnp.concatenate([inv_cos, inv_sin], 0).astype(jnp.bfloat16)
    table_four = jnp.concatenate(
        [jnp.concatenate([inv_cos.T, inv_sin.T], 1), jnp.concatenate([-inv_sin.T, inv_cos.T], 1)], 0
    ).astype(jnp.bfloat16)
    offset = jnp.abs(jnp.arange(length, dtype=jnp.float32) - length // 2)
    mask_angle = 0.5 * math.pi * (offset[:, None] + offset[None, :])
    return (table_one, table_two, table_three, table_four, jnp.cos(mask_angle), jnp.sin(mask_angle))


def detector_frame(pupil_phase, amplitude, mod_point, tables):
    table_one, table_two, table_three, table_four, mask_cos, mask_sin = tables
    pupil_size = pupil_phase.shape[0]
    length = mask_cos.shape[0]
    centred = jnp.arange(pupil_size, dtype=jnp.float32) - pupil_size // 2
    tilt_angle = 2.0 * math.pi / point_count * mod_point.astype(jnp.float32)
    tilt_phase = (
        2.0
        * math.pi
        * radius_pixels
        / length
        * (centred[:, None] * jnp.cos(tilt_angle) + centred[None, :] * jnp.sin(tilt_angle))
    )
    total_phase = pupil_phase + tilt_phase
    pupil_field = jnp.concatenate(
        [amplitude * jnp.cos(total_phase), amplitude * jnp.sin(total_phase)], 1
    ).astype(jnp.bfloat16)
    section_one = jnp.dot(table_one, pupil_field, preferred_element_type=jnp.float32)
    real_part = section_one[:length, :pupil_size] - section_one[length:, pupil_size:]
    imag_part = section_one[:length, pupil_size:] + section_one[length:, :pupil_size]
    focal_half = jnp.concatenate([real_part, imag_part], 1).astype(jnp.bfloat16)
    focal_field = jnp.dot(focal_half, table_two, preferred_element_type=jnp.float32)
    focal_real = focal_field[:, :length]
    focal_imag = focal_field[:, length:]
    masked = jnp.concatenate(
        [
            focal_real * mask_cos - focal_imag * mask_sin,
            focal_real * mask_sin + focal_imag * mask_cos,
        ],
        1,
    ).astype(jnp.bfloat16)
    section_three = jnp.dot(table_three, masked, preferred_element_type=jnp.float32)
    inverse_half = jnp.concatenate(
        [
            section_three[:length, :length] - section_three[length:, length:],
            section_three[:length, length:] + section_three[length:, :length],
        ],
        1,
    ).astype(jnp.bfloat16)
    detector_field = jnp.dot(inverse_half, table_four, preferred_element_type=jnp.float32)
    return detector_field[:, :length] ** 2 + detector_field[:, length:] ** 2


def mirror_surface(commands, act_map, gx, gy):
    actuator_grid = commands[act_map].reshape(gx.shape[1], gy.shape[1])
    rows_mapped = jnp.dot(
        gx, actuator_grid, precision=lax.Precision.HIGHEST, preferred_element_type=jnp.float32
    )
    return jnp.dot(
        rows_mapped, gy.T, precision=lax.Precision.HIGHEST, preferred_element_type=jnp.float32
    )


def body(turbulence, pupil_amp, mod_points, valid_pix, recon, gx, gy, act_map):
    pupil_size = pupil_amp.shape[0]
    length = 2 * pupil_size
    tables = optics_tables(pupil_size, length)
    screen = turbulence[0]
    mod_point = mod_points[0]
    devices_mod = lax.axis_size("mod")
    row_count = length // devices_mod
    command_total = jnp.zeros((1, act_map.shape[0]), jnp.float32)
    pupil_phase = screen
    frame_block = jnp.zeros((row_count, length), jnp.float32)
    for iteration in range(STEPS):
        frame_term = detector_frame(pupil_phase, pupil_amp, mod_point, tables) / devices_mod
        summed = lax.psum(frame_term, "mod")
        frame_block = lax.dynamic_slice_in_dim(
            summed, lax.axis_index("mod") * row_count, row_count, 0
        )
        local_index = valid_pix - lax.axis_index("mod") * (row_count * length)
        signal = frame_block.reshape(-1)[local_index].astype(jnp.bfloat16)
        signals = lax.all_gather(signal[None, :], "case", axis=0, tiled=True)
        partial_commands = lax.dot_general(
            signals, recon, (((1,), (1,)), ((), ())), preferred_element_type=jnp.float32
        )
        summed_commands = lax.psum(partial_commands, "mod")
        own_commands = lax.all_to_all(
            summed_commands, "case", split_axis=0, concat_axis=1, tiled=True
        )
        command_total = command_total + loop_gain * own_commands
        if iteration + 1 < STEPS:
            pupil_phase = screen - mirror_surface(command_total[0], act_map, gx, gy)
    return (command_total, frame_block[None])


def solution(mesh):
    return jax.shard_map(
        body,
        mesh=mesh,
        in_specs=(P("case", None, None), P(), P("mod"), P("mod"), P("case", "mod"), P(), P(), P()),
        out_specs=(P("case", None), P("case", "mod", None)),
        check_vma=False,
    )
```

profile of v0, /device:TPU:1, one launch (start us, length us, event | category | flops | bytes accessed | tf_op | source)
XLA Modules:
  0.0 1675.0 jit_solution(15463527894372798279)
XLA Ops:
  7.2 0.0 copy-start
  8.2 3.1 multiply_convert_fusion.5
  11.3 3.1 fusion.64
  14.4 9.8 fusion.39
  24.1 0.1 copy.20
  24.3 1.1 copy.21
  25.4 1.2 multiply_convert_fusion.9
  26.6 1.5 fusion.66
  28.1 0.2 fusion.49
  28.3 0.7 fusion.50
  29.0 4.7 subtract_convert_fusion.1
  33.7 0.0 copy-done.7
  33.7 0.0 copy-done.9
  33.7 1.3 fusion.15
  35.0 0.0 copy-start.1
  35.1 0.0 copy-start.3
  35.1 0.0 copy-start.5
  35.1 0.4 fusion.14
  35.4 0.6 copy-done.1
  36.1 0.2 copy-done.3
  36.3 0.2 copy-done.5
  36.4 1.3 fusion.19
  37.7 0.0 copy-start.19
  37.7 1.2 fusion.12
  38.9 267.6 %all-reduce.4 = bf16[512,512]{1,0:T(8,128)(2,1)} all-reduce(f32[512,512]{1,0:T(8,128)} %fusion.12), channel_id=1, replica_groups=mesh['case'=4,'mod'=64] {'mod'}, use_global_device_ids=true, to_apply=%region_0.1 | all-reduce | flops 262144 | bytes 1572864 | tf_op jit(solution)/shard_map/psum | solution.py:106
  306.6 0.7 dynamic-slice_bitcast_fusion
  307.3 0.0 copy-start.18
  307.3 6.8 gather_fusion
  314.1 62.2 %all-gather = bf16[4096]{0:T(1024)(128)(2,1)S(1)} all-gather(bf16[1024]{0:T(1024)(128)(2,1)S(1)} %gather_fusion), channel_id=2, replica_groups=mesh['case'=4,'mod'=64] {'case'}, dimensions={0}, use_global_device_ids=true | all-gather | bytes 10240 | tf_op jit(solution)/shard_map/all_gather | solution.py:112
  376.3 0.0 copy-done
  376.3 0.8 convolution_bitcast_fusion.1
  377.1 247.9 %psum.29 = f32[4,1,1280]{2,0,1:T(4,128)S(1)} all-reduce(f32[4,1,1280]{2,0,1:T(4,128)S(1)} %convolution_bitcast_fusion.1), channel_id=1, replica_groups=mesh['case'=4,'mod'=64] {'mod'}, use_global_device_ids=true, to_apply=%region_1.2 | all-reduce | flops 5120 | bytes 40960 | tf_op jit(solution)/shard_map/psum | solution.py:116
  625.0 0.6 copy.23
  625.6 59.2 %all-to-all-start = ((f32[4,1,1280]{2,1,0:T(1,128)}), f32[4,1,1280]{2,1,0:T(1,128)S(1)}, u32[]{:S(2)}, u32[]{:S(2)}) async-start(f32[4,1,1280]{2,1,0:T(1,128)} %copy.23), calls=%async_computation | async-start | bytes 40960 | tf_op jit(solution)/shard_map/all_to_all | solution.py:117
  684.8 0.0 all-reduce.3.cloned.1.call-start
  684.8 0.0 copy-done.18
  684.8 4.6 all-to-all-done
  689.4 28.7 %gather_fusion.1 = f32[5120]{0:T(1024)S(1)} fusion(f32[5120]{0:T(1024)S(1)} %bitcast.31, s32[5120]{0:T(1024)S(1)} %fusion.73), kind=kCustom, calls=%fused_computation.1 | custom fusion | bytes 61440 | tf_op jit(solution)/shard_map/gather | solution.py:84
  718.1 0.1 reshape.105
  718.2 1.1 fusion.85
  719.3 2.2 multiply_convert_fusion.7
  721.6 1.5 fusion.65
  723.0 0.2 fusion.47
  723.2 0.7 fusion.54
  724.0 4.7 subtract_convert_fusion
  728.7 1.3 fusion.23
  730.1 0.4 fusion.10
  730.4 0.6 copy-done.2
  731.1 0.2 copy-done.4
  731.2 0.2 copy-done.6
  731.4 1.3 fusion.27
  732.7 1.2 fusion.8
  733.8 0.0 all-reduce.3.cloned.1.call-update
  733.9 554.2 %all-reduce.3.cloned.1.call-done = f32[512,512]{1,0:T(8,128)} async-done(((f32[512,512]{1,0:T(8,128)}), f32[512,512]{1,0:T(8,128)}) %all-reduce.3.cloned.1.call-update) | async-done | bytes 1048592 | tf_op jit(solution)/shard_map/psum | solution.py:106
  1288.1 0.7 dynamic-slice_bitcast_fusion.2
  1288.8 6.8 gather_fusion.2
  1295.6 54.1 %all-gather.1 = bf16[4096]{0:T(1024)(128)(2,1)S(1)} all-gather(bf16[1024]{0:T(1024)(128)(2,1)S(1)} %gather_fusion.2), channel_id=3, replica_groups=mesh['case'=4,'mod'=64] {'case'}, dimensions={0}, use_global_device_ids=true | all-gather | bytes 10240 | tf_op jit(solution)/shard_map/all_gather | solution.py:112
  1349.8 0.8 convolution_bitcast_fusion
  1350.5 252.5 %psum.31 = f32[4,1,1280]{2,0,1:T(4,128)S(1)} all-reduce(f32[4,1,1280]{2,0,1:T(4,128)S(1)} %convolution_bitcast_fusion), channel_id=1, replica_groups=mesh['case'=4,'mod'=64] {'mod'}, use_global_device_ids=true, to_apply=%region_3.4 | all-reduce | flops 5120 | bytes 40960 | tf_op jit(solution)/shard_map/psum | solution.py:116
  1603.0 0.6 copy.26
  1603.7 59.3 %all-to-all-start.1 = ((f32[4,1,1280]{2,1,0:T(1,128)}), f32[4,1,1280]{2,1,0:T(1,128)S(1)}, u32[]{:S(2)}, u32[]{:S(2)}) async-start(f32[4,1,1280]{2,1,0:T(1,128)} %copy.26), calls=%async_computation.1 | async-start | bytes 40960 | tf_op jit(solution)/shard_map/all_to_all | solution.py:117
  1662.9 1.3 dynamic-slice_bitcast_fusion.1
  1664.2 3.3 all-to-all-done.1
  1667.6 0.6 add_multiply_fusion.2
  (34 shorter events, 0.1 us)
Async XLA Ops:
  7.2 369.1 %copy-start = (bf16[1280,1024]{1,0:T(8,128)(2,1)S(1)}, bf16[1280,1024]{1,0:T(8,128)(2,1)}, u32[]{:S(2)}) copy-start(bf16[1280,1024]{1,0:T(8,128)(2,1)} %param.12) | copy-start | bytes 7864324
  7.2 17.0 %copy-start.17 = (f32[1,256,256]{2,1,0:T(8,128)S(1)}, f32[1,256,256]{2,1,0:T(8,128)}, u32[]{:S(2)}) copy-start(f32[1,256,256]{2,1,0:T(8,128)} %param.8) | copy-start | bytes 786436
  26.6 1.7 copy-start.11
  26.6 1.7 copy-start.13
  26.6 1.7 copy-start.15
  29.0 4.7 copy-start.7
  29.0 4.7 copy-start.9
  35.0 1.0 copy-start.1
  35.1 1.2 copy-start.3
  35.1 1.3 copy-start.5
  37.7 269.6 %copy-start.19 = (s32[1024]{0:T(1024)S(1)}, s32[1024]{0:T(1024)}, u32[]{:S(2)}) copy-start(s32[1024]{0:T(1024)} %param.11) | copy-start | bytes 12292
  307.3 377.5 %copy-start.18 = (s32[5120]{0:T(1024)S(1)}, s32[5120]{0:T(1024)}, u32[]{:S(2)}) copy-start(s32[5120]{0:T(1024)} %param.15) | copy-start | bytes 61444
  625.6 63.8 %all-to-all-start = ((f32[4,1,1280]{2,1,0:T(1,128)}), f32[4,1,1280]{2,1,0:T(1,128)S(1)}, u32[]{:S(2)}, u32[]{:S(2)}) async-start(f32[4,1,1280]{2,1,0:T(1,128)} %copy.23), calls=%async_computation | async-start | bytes 40960 | tf_op jit(solution)/shard_map/all_to_all | solution.py:117
  684.8 603.3 %all-reduce.3.cloned.1.call-start = ((), (), s32[]{:S(2)}) async-start(), calls=%async_computation.2 | async-start | bytes 2097152 | tf_op jit(solution)/shard_map/psum | solution.py:106
  721.5 1.7 copy-start.12
  721.5 1.7 copy-start.14
  721.5 1.7 copy-start.16
  724.0 4.7 copy-start.8
  724.0 4.7 copy-start.10
  730.0 1.0 copy-start.2
  730.0 1.2 copy-start.4
  730.0 1.3 copy-start.6
  1603.7 63.9 %all-to-all-start.1 = ((f32[4,1,1280]{2,1,0:T(1,128)}), f32[4,1,1280]{2,1,0:T(1,128)S(1)}, u32[]{:S(2)}, u32[]{:S(2)}) async-start(f32[4,1,1280]{2,1,0:T(1,128)} %copy.26), calls=%async_computation.1 | async-start | bytes 40960 | tf_op jit(solution)/shard_map/all_to_all | solution.py:117
Sparse Core Ops, SparseCore 0:
  734.0 554.0 all-reduce.2
where the time goes:
time: 1680 us
  blocking collectives  884 us (53%)
  waiting for transfers between devices  562 us (33%)
  starting transfers between devices  118 us (7%)
  local copies, waits for them, and re-layouts  49.6 us (3%)
  other arithmetic  30.7 us (2%)
    psum x1, waiting for transfers between devices, body(): summed = lax.psum(frame_term, 'mod')  554 us
    psum x2, blocking collectives, body(): summed_commands = lax.psum(partial_commands, 'mod')  500 us
    psum x1, blocking collectives, body(): summed = lax.psum(frame_term, 'mod')  268 us
    all_to_all x2, starting transfers between devices, body(): lax.all_to_all(summed_commands, 'case', split_axis=0, concat_axis=1, tile...  118 us
    all_gather x2, blocking collectives, body(): signals = lax.all_gather(signal[None, :], 'case', axis=0, tiled=True)  116 us
  transfers between devices with their start and end apart: 3, of which 3 were waited for; matrix products, arithmetic and copies ran while one was open for 0% of the time, Pallas kernels for 0%

commit v1 on v0

--- a/solution.py
+++ b/solution.py
@@ -3,6 +3,7 @@
 import jax.numpy as jnp
 from jax import lax
 from jax.sharding import PartitionSpec as P
+from jax.lax import all_to_all, axis_size
 
 STEPS = 2
 loop_gain = 0.5
@@ -109,7 +110,15 @@
         )
         local_index = valid_pix - lax.axis_index("mod") * (row_count * length)
         signal = frame_block.reshape(-1)[local_index].astype(jnp.bfloat16)
-        signals = lax.all_gather(signal[None, :], "case", axis=0, tiled=True)
+        signals = jnp.concatenate(
+            all_to_all(
+                jnp.stack(axis_size("case") * [signal[None, :]]),
+                axis_name="case",
+                concat_axis=0,
+                split_axis=0,
+            ),
+            0,
+        )
         partial_commands = lax.dot_general(
             signals, recon, (((1,), (1,)), ((), ())), preferred_element_type=jnp.float32
         )

time: 1680 us -> 1680 us (level)
    all_to_all x0 -> x2, blocking collectives: none -> 120 us  [body(): all_to_all(jnp.stack(axis_size('case') * [signal[None, :]]), axis_name='c...]
    all_gather x2 -> x0, blocking collectives: 116 us -> none  [body(): signals = lax.all_gather(signal[None, :], 'case', axis=0, tiled=True)]
where the time goes in v1:
time: 1680 us
  blocking collectives  887 us (53%)
  waiting for transfers between devices  562 us (33%)
  starting transfers between devices  118 us (7%)
  local copies, waits for them, and re-layouts  50.1 us (3%)
  other arithmetic  32.1 us (2%)
    psum x1, waiting for transfers between devices, body(): summed = lax.psum(frame_term, 'mod')  554 us
    psum x2, blocking collectives, body(): summed_commands = lax.psum(partial_commands, 'mod')  499 us
    psum x1, blocking collectives, body(): summed = lax.psum(frame_term, 'mod')  268 us
    all_to_all x2, blocking collectives, body(): all_to_all(jnp.stack(axis_size('case') * [signal[None, :]]), axis_name='c...  120 us
    all_to_all x2, starting transfers between devices, body(): lax.all_to_all(summed_commands, 'case', split_axis=0, concat_axis=1, tile...  118 us
  transfers between devices with their start and end apart: 3, of which 3 were waited for; matrix products, arithmetic and copies ran while one was open for 0% of the time, Pallas kernels for 0%

profile of v1, /device:TPU:1, one launch (start us, length us, event | category | flops | bytes accessed | tf_op | source)
XLA Modules:
  0.0 1679.7 jit_solution(286724778800035173)
XLA Ops:
  7.2 0.0 copy-start
  8.2 3.2 multiply_convert_fusion.5
  11.3 3.1 fusion.64
  14.4 9.8 fusion.39
  24.1 0.0 copy-done.17
  24.1 0.1 copy.20
  24.3 1.1 copy.21
  25.4 1.2 multiply_convert_fusion.9
  26.6 1.5 fusion.66
  28.1 0.2 fusion.49
  28.3 0.7 fusion.50
  29.0 4.7 subtract_convert_fusion.1
  33.7 1.3 fusion.15
  35.0 0.0 copy-start.1
  35.1 0.0 copy-start.3
  35.1 0.0 copy-start.5
  35.1 0.4 fusion.14
  35.4 0.6 copy-done.1
  36.1 0.2 copy-done.3
  36.3 0.2 copy-done.5
  36.4 1.3 fusion.19
  37.7 0.0 copy-start.19
  37.7 1.2 fusion.12
  38.9 267.6 %all-reduce.4 = bf16[512,512]{1,0:T(8,128)(2,1)} all-reduce(f32[512,512]{1,0:T(8,128)} %fusion.12), channel_id=1, replica_groups=mesh['case'=4,'mod'=64] {'mod'}, use_global_device_ids=true, to_apply=%region_0.1 | all-reduce | flops 262144 | bytes 1572864 | tf_op jit(solution)/shard_map/psum | solution.py:107
  306.5 0.7 dynamic-slice_bitcast_fusion
  307.3 0.0 copy-start.18
  307.3 6.8 gather_fusion
  314.1 0.5 broadcast.197
  314.6 0.7 reduce
  315.3 64.2 %all_to_all.36 = bf16[4,2,512]{2,1,0:T(2,128)(2,1)S(1)} all-to-all(bf16[4,2,512]{2,1,0:T(2,128)(2,1)S(1)} %reshape.138), channel_id=1, replica_groups=mesh['case'=4,'mod'=64] {'case'}, dimensions={0} | all-to-all | bytes 16384 | tf_op jit(solution)/shard_map/all_to_all | solution.py:114
  379.6 0.8 convolution_bitcast_fusion.1
  380.4 247.6 %psum.29 = f32[4,1,1280]{2,0,1:T(4,128)S(1)} all-reduce(f32[4,1,1280]{2,0,1:T(4,128)S(1)} %convolution_bitcast_fusion.1), channel_id=1, replica_groups=mesh['case'=4,'mod'=64] {'mod'}, use_global_device_ids=true, to_apply=%region_1.2 | all-reduce | flops 5120 | bytes 40960 | tf_op jit(solution)/shard_map/psum | solution.py:125
  627.9 0.6 copy.23
  628.5 59.1 %all-to-all-start.1 = ((f32[4,1,1280]{2,1,0:T(1,128)}), f32[4,1,1280]{2,1,0:T(1,128)S(1)}, u32[]{:S(2)}, u32[]{:S(2)}) async-start(f32[4,1,1280]{2,1,0:T(1,128)} %copy.23), calls=%async_computation.1 | async-start | bytes 40960 | tf_op jit(solution)/shard_map/all_to_all | solution.py:126
  687.6 0.0 all-reduce.3.cloned.1.call-start
  687.7 4.6 all-to-all-done.1
  692.3 28.7 %gather_fusion.1 = f32[5120]{0:T(1024)S(1)} fusion(f32[5120]{0:T(1024)S(1)} %bitcast.35, s32[5120]{0:T(1024)S(1)} %fusion.73), kind=kCustom, calls=%fused_computation.1 | custom fusion | bytes 61440 | tf_op jit(solution)/shard_map/gather | solution.py:85
  721.0 0.1 reshape.108
  721.1 1.1 fusion.89
  722.2 2.2 multiply_convert_fusion.7
  724.4 1.5 fusion.65
  725.9 0.2 fusion.47
  726.1 0.7 fusion.54
  726.9 4.7 subtract_convert_fusion
  731.6 1.3 fusion.23
  732.9 0.4 fusion.10
  733.3 0.6 copy-done.2
  734.0 0.2 copy-done.4
  734.1 0.2 copy-done.6
  734.3 1.3 fusion.27
  735.5 1.2 fusion.8
  736.8 0.0 all-reduce.3.cloned.1.call-update
  736.8 554.2 %all-reduce.3.cloned.1.call-done = f32[512,512]{1,0:T(8,128)} async-done(((f32[512,512]{1,0:T(8,128)}), f32[512,512]{1,0:T(8,128)}) %all-reduce.3.cloned.1.call-update) | async-done | bytes 1048592 | tf_op jit(solution)/shard_map/psum | solution.py:107
  1291.0 0.7 dynamic-slice_bitcast_fusion.2
  1291.7 6.8 gather_fusion.2
  1298.5 0.7 reduce.1
  1299.3 56.0 %all_to_all.37 = bf16[4,2,512]{2,1,0:T(2,128)(2,1)S(1)} all-to-all(bf16[4,2,512]{2,1,0:T(2,128)(2,1)S(1)} %reshape.140), channel_id=1, replica_groups=mesh['case'=4,'mod'=64] {'case'}, dimensions={0} | all-to-all | bytes 16384 | tf_op jit(solution)/shard_map/all_to_all | solution.py:114
  1355.3 0.8 convolution_bitcast_fusion
  1356.0 251.6 %psum.31 = f32[4,1,1280]{2,0,1:T(4,128)S(1)} all-reduce(f32[4,1,1280]{2,0,1:T(4,128)S(1)} %convolution_bitcast_fusion), channel_id=1, replica_groups=mesh['case'=4,'mod'=64] {'mod'}, use_global_device_ids=true, to_apply=%region_3.4 | all-reduce | flops 5120 | bytes 40960 | tf_op jit(solution)/shard_map/psum | solution.py:125
  1607.6 0.6 copy.26
  1608.2 59.4 %all-to-all-start.3 = ((f32[4,1,1280]{2,1,0:T(1,128)}), f32[4,1,1280]{2,1,0:T(1,128)S(1)}, u32[]{:S(2)}, u32[]{:S(2)}) async-start(f32[4,1,1280]{2,1,0:T(1,128)} %copy.26), calls=%async_computation.3 | async-start | bytes 40960 | tf_op jit(solution)/shard_map/all_to_all | solution.py:126
  1667.6 1.3 dynamic-slice_bitcast_fusion.1
  1668.9 3.3 all-to-all-done.3
  1672.2 0.6 add_multiply_fusion.2
  (41 shorter events, 0.2 us)
Async XLA Ops:
  7.2 372.4 %copy-start = (bf16[1280,1024]{1,0:T(8,128)(2,1)S(1)}, bf16[1280,1024]{1,0:T(8,128)(2,1)}, u32[]{:S(2)}) copy-start(bf16[1280,1024]{1,0:T(8,128)(2,1)} %param.12) | copy-start | bytes 7864324
  7.2 17.0 %copy-start.17 = (f32[1,256,256]{2,1,0:T(8,128)S(1)}, f32[1,256,256]{2,1,0:T(8,128)}, u32[]{:S(2)}) copy-start(f32[1,256,256]{2,1,0:T(8,128)} %param.8) | copy-start | bytes 786436
  26.6 1.7 copy-start.11
  26.6 1.7 copy-start.13
  26.6 1.7 copy-start.15
  29.0 4.7 copy-start.7
  29.0 4.7 copy-start.9
  35.0 1.0 copy-start.1
  35.1 1.2 copy-start.3
  35.1 1.3 copy-start.5
  37.7 269.6 %copy-start.19 = (s32[1024]{0:T(1024)S(1)}, s32[1024]{0:T(1024)}, u32[]{:S(2)}) copy-start(s32[1024]{0:T(1024)} %param.11) | copy-start | bytes 12292
  307.3 380.4 %copy-start.18 = (s32[5120]{0:T(1024)S(1)}, s32[5120]{0:T(1024)}, u32[]{:S(2)}) copy-start(s32[5120]{0:T(1024)} %param.15) | copy-start | bytes 61444
  628.5 63.8 %all-to-all-start.1 = ((f32[4,1,1280]{2,1,0:T(1,128)}), f32[4,1,1280]{2,1,0:T(1,128)S(1)}, u32[]{:S(2)}, u32[]{:S(2)}) async-start(f32[4,1,1280]{2,1,0:T(1,128)} %copy.23), calls=%async_computation.1 | async-start | bytes 40960 | tf_op jit(solution)/shard_map/all_to_all | solution.py:126
  687.6 603.3 %all-reduce.3.cloned.1.call-start = ((), (), s32[]{:S(2)}) async-start(), calls=%async_computation.4 | async-start | bytes 2097152 | tf_op jit(solution)/shard_map/psum | solution.py:107
  724.4 1.7 copy-start.12
  724.4 1.7 copy-start.14
  724.4 1.7 copy-start.16
  726.9 4.7 copy-start.8
  726.9 4.7 copy-start.10
  732.9 1.0 copy-start.2
  732.9 1.2 copy-start.4
  732.9 1.3 copy-start.6
  1608.2 64.0 %all-to-all-start.3 = ((f32[4,1,1280]{2,1,0:T(1,128)}), f32[4,1,1280]{2,1,0:T(1,128)S(1)}, u32[]{:S(2)}, u32[]{:S(2)}) async-start(f32[4,1,1280]{2,1,0:T(1,128)} %copy.26), calls=%async_computation.3 | async-start | bytes 40960 | tf_op jit(solution)/shard_map/all_to_all | solution.py:126
Sparse Core Ops, SparseCore 0:
  736.9 554.0 all-reduce.2
